TPU v7x, 256 devices: a whole 4x4x8 slice. The times are simulated.
256 devices in a mesh: particle: 16 (over z_hi, y), space: 16 (over x, z_lo, core).
Axes of the slice: x: 4, y: 4, z: 8 (z_hi: 4, z_lo: 2; z = z_hi * 2 + z_lo), core: 2. Of those that a mesh axis runs over, the one named last changes fastest.
Arguments:
- ensemble: float32 [16, 13, 512, 1024], P('particle', None, 'space'), may hold values from -6 to 6
- ancestors: int32 [16], replicated, may hold values from 0 to 15
- depth_levels: int32 [512, 1024], P('space'), may hold values from 0 to 4
- level_coefs: float32 [3, 4], replicated, may hold values from 0.25 to 1
- altimetry: float32 [3, 64, 512], P(None, 'particle', 'space'), may hold values from -6 to 6
- obs_rows: int32 [3, 64], replicated, may hold values from 0 to 1023, as said below
Outputs:
- forecast: float32 [16, 13, 512, 1024], P('particle', None, 'space')
Inputs may be any that keep to these rules, and one draw needn't show every extreme that they name: `obs_rows`: within one step the indices are distinct.
All inputs are finite; a program needn't handle non-finite values.
Results may differ from a plain program's by a relative error of at most 0.00013.
Values sent between devices are 32-bit elements; how exact they have to be, the bound alone decides.
A program may use at most 128 MiB of HBM per device.

v0:
```python
import jax
import jax.numpy as jnp
from jax import lax
from jax.sharding import PartitionSpec as P

STEPS = 3
DT = 0.2
CORIOLIS = 0.5
GRAVITY = 1.0
NUDGE = 0.5


def with_halo(block, sides, width):
    for axis, dim in sides:
        count = lax.axis_size(axis)
        forward = [(i, i + 1) for i in range(count - 1)]
        forward.append((count - 1, 0))
        backward = [(target, source) for source, target in forward]
        low = lax.ppermute(
            lax.slice_in_dim(block, block.shape[dim] - width, None, axis=dim), axis, forward
        )
        high = lax.ppermute(lax.slice_in_dim(block, 0, width, axis=dim), axis, backward)
        block = jnp.concatenate([low, block, high], axis=dim)
    return block


def pad_second(field):
    return jnp.pad(field, [(0, 0)] * (field.ndim - 1) + [(1, 1)])


def gradients(wide):
    center = wide[:, 1:-1]
    east = wide[:, 2:]
    west = wide[:, :-2]
    padded = pad_second(center)
    ddx = (east - west) * 0.5
    ddy = (padded[..., 2:] - padded[..., :-2]) * 0.5
    laplace = east + west + padded[..., 2:] + padded[..., :-2] - 4.0 * center
    return (center, ddx, ddy, laplace)


def widen_state(field):
    return with_halo(field, (("space", 1),), 1)


def widen_surface(field):
    return with_halo(field, (("space", 1),), 1)


def level_terms(coefs):
    thick = coefs[0][:, None, None]
    visc = 0.2 * coefs[1][:, None, None]
    kappa = 0.2 * coefs[2][:, None, None]
    return (thick, visc, kappa)


def finish(center, ddx, ddy, laplace, masks, visc, kappa, grad_x, grad_y, height_two):
    levels = masks.shape[0]
    east_vel = center[:levels]
    north_vel = center[levels : 2 * levels]
    temper = center[2 * levels : 3 * levels]
    east_new = masks * (
        east_vel + DT * (CORIOLIS * north_vel - GRAVITY * grad_x + visc * laplace[:levels])
    )
    north_new = masks * (
        north_vel
        + DT * (-CORIOLIS * east_vel - GRAVITY * grad_y + visc * laplace[levels : 2 * levels])
    )
    temper_new = masks * (
        temper
        + DT
        * (
            kappa * laplace[2 * levels : 3 * levels]
            - east_vel * ddx[2 * levels : 3 * levels]
            - north_vel * ddy[2 * levels : 3 * levels]
        )
    )
    return jnp.concatenate([east_new, north_new, temper_new, height_two[None]], axis=0)


def one_step(state, masks, coefs, target, hit):
    levels = masks.shape[0]
    surface = masks[0]
    center, ddx, ddy, laplace = gradients(widen_state(state))
    height = center[3 * levels]
    thick, visc, kappa = level_terms(coefs)
    spread = ddx[:levels] + ddy[levels : 2 * levels]
    height_one = surface * (height - DT * jnp.sum(thick * masks * spread, axis=0))
    height_two = surface * (height_one + NUDGE * hit * (target - height_one))
    unused, grad_x, grad_y, unused_lap = gradients(widen_surface(height_two[None]))
    return finish(center, ddx, ddy, laplace, masks, visc, kappa, grad_x, grad_y, height_two)


def per_device(ensemble, ancestors, depth_levels, level_coefs, altimetry, obs_rows):
    levels = level_coefs.shape[1]
    width_y = ensemble.shape[3]
    mine = ancestors[lax.axis_index("particle")]
    piece = lax.all_gather(ensemble, "particle", axis=0, tiled=True)
    count = piece.shape[0]
    inside = (mine >= 0) & (mine < count)
    chosen = lax.dynamic_index_in_dim(piece, jnp.clip(mine, 0, count - 1), 0, keepdims=False)
    state = jnp.where(inside, chosen, jnp.zeros(ensemble.shape[1:], jnp.float32))
    level_ids = jnp.arange(levels, dtype=jnp.int32)
    masks = (level_ids[:, None, None] < depth_levels[None]).astype(jnp.float32)
    full_mask = jnp.concatenate([masks, masks, masks, masks[:1]], axis=0)
    state = state * full_mask
    columns = jnp.arange(width_y, dtype=jnp.int32)
    for step in range(STEPS):
        lines = lax.all_gather(altimetry[step], "particle", axis=0, tiled=True)
        onehot = (obs_rows[step][:, None] == columns[None, :]).astype(jnp.float32)
        target = jnp.dot(
            lines.T, onehot, precision=lax.Precision.HIGHEST, preferred_element_type=jnp.float32
        )
        hit = jnp.sum(onehot, axis=0)[None, :]
        state = one_step(state, masks, level_coefs, target, hit)
    return state[None]


def solution(mesh):
    in_specs = (
        P("particle", None, "space", None),
        P(),
        P("space", None),
        P(),
        P(None, "particle", "space"),
        P(),
    )
    out_specs = P("particle", None, "space", None)
    return jax.shard_map(
        per_device, mesh=mesh, in_specs=in_specs, out_specs=out_specs, check_vma=False
    )
```

profile of v0, /device:TPU:8, one launch (start us, length us, event | category | flops | bytes accessed | tf_op | source)
XLA Modules:
  0.0 483.3 jit_solution(3686461918665860004)
XLA Ops:
  6.6 0.7 all-gather.5.cloned.1.call-update
  7.3 0.6 dynamic_slice.7
  9.9 0.1 convert_reduce_fusion.2
  10.1 312.0 %all-gather.5.cloned.1.call-done = f32[16,13,32,1024]{3,2,1,0:T(8,128)} async-done(((f32[1,13,32,1024]{3,2,1,0:T(8,128)}), f32[16,13,32,1024]{3,2,1,0:T(8,128)}) %all-gather.5.cloned.1.call-update) | async-done | bytes 27262992 | tf_op jit(solution)/shard_map/all_gather | solution.py:98
  322.1 1.7 maximum_multiply_fusion
  323.9 0.1 collective-permute-start
  324.0 0.5 collective-permute-start.1
  324.5 40.4 %all-gather = f32[1,64,32]{2,0,1:T(1,128)S(1)} all-gather(f32[1,4,32]{2,0,1:T(1,128)S(1)} %bitcast.108), channel_id=2, replica_groups=mesh['particle'=16,'space'=16] {'particle'}, dimensions={1}, use_global_device_ids=true | all-gather | bytes 8704 | tf_op jit(solution)/shard_map/all_gather | solution.py:109
  364.9 1.8 multiply_subtract_fusion.2
  366.7 0.2 fusion.13
  366.9 0.3 fusion.3
  367.2 0.1 collective-permute-start.2
  367.3 0.5 collective-permute-start.3
  367.8 0.1 convert_reduce_fusion.1
  367.9 0.7 collective-permute-done.2
  368.6 3.9 collective-permute-done.3
  372.5 0.1 fusion.73
  372.6 0.6 fusion.54
  373.3 0.2 pad_maximum_fusion.18
  373.5 0.1 collective-permute-start.4
  373.6 0.5 collective-permute-start.5
  374.1 43.4 %all-gather.1 = f32[1,64,32]{2,0,1:T(1,128)S(1)} all-gather(f32[1,4,32]{2,0,1:T(1,128)S(1)} %bitcast.107), channel_id=3, replica_groups=mesh['particle'=16,'space'=16] {'particle'}, dimensions={1}, use_global_device_ids=true | all-gather | bytes 8704 | tf_op jit(solution)/shard_map/all_gather | solution.py:109
  417.5 0.4 subtract_multiply_fusion.3
  417.9 2.1 multiply_subtract_fusion.1
  420.0 0.5 fusion.32
  420.6 0.3 fusion.7
  420.9 0.1 collective-permute-start.6
  421.0 0.5 collective-permute-start.7
  421.5 0.1 convert_reduce_fusion
  421.6 0.7 collective-permute-done.6
  422.3 4.1 collective-permute-done.7
  426.4 0.1 fusion.70
  426.5 0.4 fusion.41
  426.9 0.2 pad_maximum_fusion.19
  427.2 0.1 collective-permute-start.8
  427.3 0.5 collective-permute-start.9
  427.8 38.1 %all-gather.2 = f32[1,64,32]{2,0,1:T(1,128)S(1)} all-gather(f32[1,4,32]{2,0,1:T(1,128)S(1)} %bitcast.106), channel_id=4, replica_groups=mesh['particle'=16,'space'=16] {'particle'}, dimensions={1}, use_global_device_ids=true | all-gather | bytes 8704 | tf_op jit(solution)/shard_map/all_gather | solution.py:109
  465.9 0.4 subtract_multiply_fusion.1
  466.4 2.1 multiply_subtract_fusion
  468.4 0.5 fusion.19
  469.0 0.3 fusion.12
  469.3 0.1 collective-permute-start.10
  469.4 0.5 collective-permute-start.11
  469.9 0.8 collective-permute-done.10
  470.7 3.9 collective-permute-done.11
  474.6 0.1 fusion.67
  474.7 0.4 fusion.28
  475.1 1.3 maximum_bitcast_fusion
  (31 shorter events, 0.4 us)
Async XLA Ops:
  6.5 0.7 copy-start.4
  6.5 3.3 copy-start
  6.5 3.4 copy-start.2
  6.5 3.5 copy-start.1
  6.5 315.6 %all-gather.5.cloned.1.call-start = ((), (), s32[]{:S(2)}) async-start(), calls=%async_computation | async-start | bytes 28966912 | tf_op jit(solution)/shard_map/all_gather | solution.py:98
  322.1 2.4 copy-start.3
  323.9 41.0 %collective-permute-start = (f32[13,1,1024]{2,1,0:T(1,128)S(1)}, f32[13,1,1024]{2,1,0:T(1,128)S(1)}, u32[]{:S(2)}, u32[]{:S(2)}) collective-permute-start(f32[13,1,1024]{2,1,0:T(1,128)S(1)} %get-tuple-element.28), channel_id=1, source_target_pairs={{1,0},{2,1},{3,2},{4,3},{5,4},{6,5},{7,6},{8,7},{9,8},{10,9},{11,1... | collective-permute-start | bytes 159752 | tf_op jit(solution)/shard_map/ppermute | solution.py:22
  324.0 40.9 %collective-permute-start.1 = (f32[13,1,1024]{2,1,0:T(1,128)S(1)}, f32[13,1,1024]{2,1,0:T(1,128)S(1)}, u32[]{:S(2)}, u32[]{:S(2)}) collective-permute-start(f32[13,1,1024]{2,1,0:T(1,128)S(1)} %get-tuple-element.27), channel_id=1, source_target_pairs={{0,1},{1,2},{2,3},{3,4},{4,5},{5,6},{6,7},{7,8},{8,9},{9,10},{10,1... | collective-permute-start | bytes 159752 | tf_op jit(solution)/shard_map/ppermute | solution.py:19
  367.2 1.4 collective-permute-start.2
  367.3 5.2 %collective-permute-start.3 = (f32[1,1,1024]{2,1,0:T(1,128)S(1)}, f32[1,1,1024]{2,1,0:T(1,128)S(1)}, u32[]{:S(2)}, u32[]{:S(2)}) collective-permute-start(f32[1,1,1024]{2,1,0:T(1,128)S(1)} %get-tuple-element.40), channel_id=1, source_target_pairs={{0,1},{1,2},{2,3},{3,4},{4,5},{5,6},{6,7},{7,8},{8,9},{9,10},{10,1... | collective-permute-start | bytes 12296 | tf_op jit(solution)/shard_map/ppermute | solution.py:19
  373.5 43.9 %collective-permute-start.4 = (f32[13,1,1024]{2,1,0:T(1,128)S(1)}, f32[13,1,1024]{2,1,0:T(1,128)S(1)}, u32[]{:S(2)}, u32[]{:S(2)}) collective-permute-start(f32[13,1,1024]{2,1,0:T(1,128)S(1)} %get-tuple-element.25), channel_id=1, source_target_pairs={{1,0},{2,1},{3,2},{4,3},{5,4},{6,5},{7,6},{8,7},{9,8},{10,9},{11,1... | collective-permute-start | bytes 159752 | tf_op jit(solution)/shard_map/ppermute | solution.py:22
  373.6 43.9 %collective-permute-start.5 = (f32[13,1,1024]{2,1,0:T(1,128)S(1)}, f32[13,1,1024]{2,1,0:T(1,128)S(1)}, u32[]{:S(2)}, u32[]{:S(2)}) collective-permute-start(f32[13,1,1024]{2,1,0:T(1,128)S(1)} %get-tuple-element.24), channel_id=1, source_target_pairs={{0,1},{1,2},{2,3},{3,4},{4,5},{5,6},{6,7},{7,8},{8,9},{9,10},{10,1... | collective-permute-start | bytes 159752 | tf_op jit(solution)/shard_map/ppermute | solution.py:19
  420.9 1.4 collective-permute-start.6
  421.0 5.4 %collective-permute-start.7 = (f32[1,1,1024]{2,1,0:T(1,128)S(1)}, f32[1,1,1024]{2,1,0:T(1,128)S(1)}, u32[]{:S(2)}, u32[]{:S(2)}) collective-permute-start(f32[1,1,1024]{2,1,0:T(1,128)S(1)} %get-tuple-element.36), channel_id=1, source_target_pairs={{0,1},{1,2},{2,3},{3,4},{4,5},{5,6},{6,7},{7,8},{8,9},{9,10},{10,1... | collective-permute-start | bytes 12296 | tf_op jit(solution)/shard_map/ppermute | solution.py:19
  427.2 38.7 %collective-permute-start.8 = (f32[13,1,1024]{2,1,0:T(1,128)S(1)}, f32[13,1,1024]{2,1,0:T(1,128)S(1)}, u32[]{:S(2)}, u32[]{:S(2)}) collective-permute-start(f32[13,1,1024]{2,1,0:T(1,128)S(1)} %get-tuple-element.21), channel_id=1, source_target_pairs={{1,0},{2,1},{3,2},{4,3},{5,4},{6,5},{7,6},{8,7},{9,8},{10,9},{11,1... | collective-permute-start | bytes 159752 | tf_op jit(solution)/shard_map/ppermute | solution.py:22
  427.3 38.6 %collective-permute-start.9 = (f32[13,1,1024]{2,1,0:T(1,128)S(1)}, f32[13,1,1024]{2,1,0:T(1,128)S(1)}, u32[]{:S(2)}, u32[]{:S(2)}) collective-permute-start(f32[13,1,1024]{2,1,0:T(1,128)S(1)} %get-tuple-element.20), channel_id=1, source_target_pairs={{0,1},{1,2},{2,3},{3,4},{4,5},{5,6},{6,7},{7,8},{8,9},{9,10},{10,1... | collective-permute-start | bytes 159752 | tf_op jit(solution)/shard_map/ppermute | solution.py:19
  469.3 1.4 collective-permute-start.10
  469.4 5.2 %collective-permute-start.11 = (f32[1,1,1024]{2,1,0:T(1,128)S(1)}, f32[1,1,1024]{2,1,0:T(1,128)S(1)}, u32[]{:S(2)}, u32[]{:S(2)}) collective-permute-start(f32[1,1,1024]{2,1,0:T(1,128)S(1)} %get-tuple-element.32), channel_id=1, source_target_pairs={{0,1},{1,2},{2,3},{3,4},{4,5},{5,6},{6,7},{7,8},{8,9},{9,10},{10,1... | collective-permute-start | bytes 12296 | tf_op jit(solution)/shard_map/ppermute | solution.py:19
Sparse Core Ops, SparseCore 0:
  9.8 312.2 all-gather.4
where the time goes:
time: 483 us
  waiting for transfers between devices  327 us (68%)
  blocking collectives  122 us (25%)
  between operations  15.7 us (3%)
  other arithmetic  13.6 us (3%)
    all_gather x1, waiting for transfers between devices, per_device(): piece = lax.all_gather(ensemble, 'particle', axis=0, tiled=True)  312 us
    all_gather x3, blocking collectives, per_device(): lines = lax.all_gather(altimetry[step], 'particle', axis=0, tiled=True)  122 us
    ppermute x6, waiting for transfers between devices, with_halo(): lax.ppermute(lax.slice_in_dim(block, block.shape[dim] - width, None, axis...  11.9 us
  transfers between devices with their start and end apart: 13, of which 7 were waited for; matrix products, arithmetic and copies ran while one was open for 0% of the time, Pallas kernels for 0%

commit v1 on v0

--- a/solution.py
+++ b/solution.py
@@ -106,7 +106,12 @@
     state = state * full_mask
     columns = jnp.arange(width_y, dtype=jnp.int32)
     for step in range(STEPS):
-        lines = lax.all_gather(altimetry[step], "particle", axis=0, tiled=True)
+        lines = jnp.concatenate(
+            lax.all_to_all(
+                jnp.stack([altimetry[step]] * lax.axis_size("particle")), "particle", 0, 0
+            ),
+            axis=0,
+        )
         onehot = (obs_rows[step][:, None] == columns[None, :]).astype(jnp.float32)
         target = jnp.dot(
             lines.T, onehot, precision=lax.Precision.HIGHEST, preferred_element_type=jnp.float32

time: 483 us -> 405 us (0.84)
  blocking collectives: 122 us -> 0 us
  starting transfers between devices: 3.51 us -> 39.3 us
  waiting for transfers between devices: 327 us -> 319 us
  local copies, waits for them, and re-layouts: 0.89 us -> 8.42 us
  other arithmetic: 13.6 us -> 18.8 us
    all_gather x3 -> x0, blocking collectives: 122 us -> none  [per_device(): lines = lax.all_gather(altimetry[step], 'particle', axis=0, tiled=True)]
    all_to_all x0 -> x3, starting transfers between devices: none -> 30.4 us  [per_device(): lax.all_to_all(jnp.stack([altimetry[step]] * lax.axis_size('particle')),...]
    all_gather x1, waiting for transfers between devices: 312 us -> 299 us  [per_device(): piece = lax.all_gather(ensemble, 'particle', axis=0, tiled=True)]
    ppermute x6, starting transfers between devices: 0.5 us -> 7.29 us  [with_halo(): lax.ppermute(lax.slice_in_dim(block, 0, width, axis=dim), axis, backward)]
    unnamed x10 -> x44, local copies, waits for them, and re-layouts: 0.02 us -> 5.1 us
  transfers between devices with their start and end apart: 13 -> 16, of which waited for: 7 -> 9; matrix products, arithmetic and copies ran while one was open for 0% -> 6% of each run, Pallas kernels for 0% -> 0%
where the time goes in v1:
time: 405 us; the launch traced here: 404 us
  waiting for transfers between devices  319 us (79%)
  starting transfers between devices  39.3 us (10%)
  other arithmetic  18.8 us (5%)
  between operations  15.7 us (4%)
  local copies, waits for them, and re-layouts  8.42 us (2%)
    all_gather x1, waiting for transfers between devices, per_device(): piece = lax.all_gather(ensemble, 'particle', axis=0, tiled=True)  299 us
    all_to_all x3, starting transfers between devices, per_device(): lax.all_to_all(jnp.stack([altimetry[step]] * lax.axis_size('particle')),...  30.4 us
    ppermute x6, waiting for transfers between devices, with_halo(): lax.ppermute(lax.slice_in_dim(block, block.shape[dim] - width, None, axis...  15.2 us
  transfers between devices with their start and end apart: 16, of which 9 were waited for; matrix products, arithmetic and copies ran while one was open for 6% of the time, Pallas kernels for 0%

profile of v1, /device:TPU:8, one launch (start us, length us, event | category | flops | bytes accessed | tf_op | source)
XLA Modules:
  0.0 403.9 jit_solution(11025495556610117492)
XLA Ops:
  6.6 0.7 all-gather.2.cloned.1.call-update
  7.3 0.7 reshape.66
  8.0 11.6 %all-to-all-start = ((f32[16,1,128]{2,1,0:T(1,128)}), f32[16,1,128]{2,1,0:T(1,128)S(1)}, u32[]{:S(2)}, u32[]{:S(2)}) async-start(f32[16,1,128]{2,1,0:T(1,128)} %reshape.66), calls=%async_computation | async-start | bytes 16384 | tf_op jit(solution)/shard_map/all_to_all | solution.py:110
  19.6 0.6 dynamic_slice.7
  22.1 0.6 slice_bitcast_fusion.6
  22.9 299.2 %all-gather.2.cloned.1.call-done = f32[16,13,32,1024]{3,2,1,0:T(8,128)} async-done(((f32[1,13,32,1024]{3,2,1,0:T(8,128)}), f32[16,13,32,1024]{3,2,1,0:T(8,128)}) %all-gather.2.cloned.1.call-update) | async-done | bytes 27262992 | tf_op jit(solution)/shard_map/all_gather | solution.py:98
  322.1 1.7 maximum_multiply_fusion
  324.0 0.5 collective-permute-start.1
  324.5 0.6 multiply_bitcast_fusion.1
  325.1 0.7 reshape.64
  325.8 9.2 %all-to-all-start.1 = ((f32[16,1,128]{2,1,0:T(1,128)}), f32[16,1,128]{2,1,0:T(1,128)S(1)}, u32[]{:S(2)}, u32[]{:S(2)}) async-start(f32[16,1,128]{2,1,0:T(1,128)} %reshape.64), calls=%async_computation.1 | async-start | bytes 16384 | tf_op jit(solution)/shard_map/all_to_all | solution.py:110
  335.0 0.5 broadcast.147
  335.5 0.7 reduce.2
  336.3 1.8 multiply_subtract_fusion.2
  338.4 0.3 fusion.3
  338.7 3.4 collective-permute-start.2
  342.2 1.2 collective-permute-done.2
  343.4 3.8 collective-permute-done.3
  347.4 0.6 fusion.54
  348.1 0.7 fusion.80
  348.9 0.5 collective-permute-start.5
  349.4 0.6 broadcast_multiply_fusion.1
  350.0 0.6 stack.11
  350.6 1.4 reshape.62
  352.0 9.6 %all-to-all-start.2 = ((f32[16,1,128]{2,1,0:T(1,128)}), f32[16,1,128]{2,1,0:T(1,128)}, u32[]{:S(2)}, u32[]{:S(2)}) async-start(f32[16,1,128]{2,1,0:T(1,128)} %reshape.62), calls=%async_computation.2 | async-start | bytes 16384 | tf_op jit(solution)/shard_map/all_to_all | solution.py:110
  361.7 0.7 reduce.1
  362.3 0.7 reshape.65
  363.0 1.3 subtract_multiply_fusion.3
  364.3 2.8 multiply_subtract_fusion.1
  367.2 0.5 fusion.32
  367.9 1.2 fusion.7
  369.1 3.1 collective-permute-start.6
  372.3 1.2 collective-permute-done.6
  373.5 3.9 collective-permute-done.7
  377.5 0.4 fusion.41
  378.0 1.2 copy-done
  379.4 0.5 collective-permute-start.9
  379.9 1.4 reduce
  381.4 3.7 collective-permute-done.9
  385.1 0.4 subtract_multiply_fusion.1
  385.5 2.0 multiply_subtract_fusion
  387.6 0.5 fusion.19
  388.1 1.2 fusion.12
  389.3 0.7 collective-permute-start.10
  390.0 1.3 collective-permute-done.10
  391.4 3.8 collective-permute-done.11
  395.3 0.4 fusion.28
  395.7 1.4 maximum_bitcast_fusion
  (75 shorter events, 2.2 us)
Async XLA Ops:
  6.5 0.7 copy-start.12
  6.5 13.0 %copy-start.18 = (s32[16]{0:T(128)S(1)}, s32[16]{0:T(128)}, u32[]{:S(2)}) copy-start(s32[16]{0:T(128)} %param.7) | copy-start | bytes 196
  6.5 15.5 %copy-start.2 = (s32[32,1024]{1,0:T(8,128)S(1)}, s32[32,1024]{1,0:T(8,128)}, u32[]{:S(2)}) copy-start(s32[32,1024]{1,0:T(8,128)} %param.8) | copy-start | bytes 393220
  6.5 15.6 %copy-start.16 = (s32[3,64]{1,0:T(4,128)S(1)}, s32[3,64]{1,0:T(4,128)}, u32[]{:S(2)}) copy-start(s32[3,64]{1,0:T(4,128)} %param.11) | copy-start | bytes 2308
  6.5 315.6 %all-gather.2.cloned.1.call-start = ((), (), s32[]{:S(2)}) async-start(), calls=%async_computation.3 | async-start | bytes 28966912 | tf_op jit(solution)/shard_map/all_gather | solution.py:98
  8.0 317.8 %all-to-all-start = ((f32[16,1,128]{2,1,0:T(1,128)}), f32[16,1,128]{2,1,0:T(1,128)S(1)}, u32[]{:S(2)}, u32[]{:S(2)}) async-start(f32[16,1,128]{2,1,0:T(1,128)} %reshape.66), calls=%async_computation | async-start | bytes 16384 | tf_op jit(solution)/shard_map/all_to_all | solution.py:110
  22.1 316.3 %copy-start.3 = (f32[4,32,1024]{2,1,0:T(8,128)}, f32[4,32,1024]{2,1,0:T(8,128)S(1)}, u32[]{:S(2)}) copy-start(f32[4,32,1024]{2,1,0:T(8,128)S(1)} %fusion.55) | copy-start | bytes 1572868
  22.8 319.3 %copy-start.14 = (s32[64]{0:T(128)}, s32[64]{0:T(128)S(1)}, u32[]{:S(2)}) copy-start(s32[64]{0:T(128)S(1)} %get-tuple-element.49) | copy-start | bytes 772
  322.1 2.4 copy-start.17
  323.9 12.4 %collective-permute-start = (f32[13,1,1024]{2,1,0:T(1,128)S(1)}, f32[13,1,1024]{2,1,0:T(1,128)S(1)}, u32[]{:S(2)}, u32[]{:S(2)}) collective-permute-start(f32[13,1,1024]{2,1,0:T(1,128)S(1)} %get-tuple-element.28), channel_id=1, source_target_pairs={{1,0},{2,1},{3,2},{4,3},{5,4},{6,5},{7,6},{8,7},{9,8},{10,9},{11,1... | collective-permute-start | bytes 159752 | tf_op jit(solution)/shard_map/ppermute | solution.py:22
  324.0 12.3 %collective-permute-start.1 = (f32[13,1,1024]{2,1,0:T(1,128)S(1)}, f32[13,1,1024]{2,1,0:T(1,128)S(1)}, u32[]{:S(2)}, u32[]{:S(2)}) collective-permute-start(f32[13,1,1024]{2,1,0:T(1,128)S(1)} %get-tuple-element.27), channel_id=1, source_target_pairs={{0,1},{1,2},{2,3},{3,4},{4,5},{5,6},{6,7},{7,8},{8,9},{9,10},{10,1... | collective-permute-start | bytes 159752 | tf_op jit(solution)/shard_map/ppermute | solution.py:19
  325.1 13.1 %copy-start.8 = (f32[4]{0:T(128)}, f32[4]{0:T(128)S(1)}, u32[]{:S(2)}) copy-start(f32[4]{0:T(128)S(1)} %get-tuple-element.45) | copy-start | bytes 52
  325.8 26.3 %all-to-all-start.1 = ((f32[16,1,128]{2,1,0:T(1,128)}), f32[16,1,128]{2,1,0:T(1,128)S(1)}, u32[]{:S(2)}, u32[]{:S(2)}) async-start(f32[16,1,128]{2,1,0:T(1,128)} %reshape.64), calls=%async_computation.1 | async-start | bytes 16384 | tf_op jit(solution)/shard_map/all_to_all | solution.py:110
  338.2 9.2 %copy-start.6 = (f32[4]{0:T(128)S(1)}, f32[4]{0:T(128)}, u32[]{:S(2)}) copy-start(f32[4]{0:T(128)} %get-tuple-element.44) | copy-start | bytes 52
  338.2 9.2 %copy-start.10 = (f32[4]{0:T(128)S(1)}, f32[4]{0:T(128)}, u32[]{:S(2)}) copy-start(f32[4]{0:T(128)} %get-tuple-element.46) | copy-start | bytes 52
  338.7 4.7 %collective-permute-start.2 = (f32[1,1,1024]{2,1,0:T(1,128)S(1)}, f32[1,1,1024]{2,1,0:T(1,128)S(1)}, u32[]{:S(2)}, u32[]{:S(2)}) collective-permute-start(f32[1,1,1024]{2,1,0:T(1,128)S(1)} %get-tuple-element.39), channel_id=1, source_target_pairs={{1,0},{2,1},{3,2},{4,3},{5,4},{6,5},{7,6},{8,7},{9,8},{10,9},{11,1... | collective-permute-start | bytes 12296 | tf_op jit(solution)/shard_map/ppermute | solution.py:22
  342.1 5.1 %collective-permute-start.3 = (f32[1,1,1024]{2,1,0:T(1,128)S(1)}, f32[1,1,1024]{2,1,0:T(1,128)S(1)}, u32[]{:S(2)}, u32[]{:S(2)}) collective-permute-start(f32[1,1,1024]{2,1,0:T(1,128)S(1)} %get-tuple-element.40), channel_id=1, source_target_pairs={{0,1},{1,2},{2,3},{3,4},{4,5},{5,6},{6,7},{7,8},{8,9},{9,10},{10,1... | collective-permute-start | bytes 12296 | tf_op jit(solution)/shard_map/ppermute | solution.py:19
  348.9 14.1 %collective-permute-start.4 = (f32[13,1,1024]{2,1,0:T(1,128)}, f32[13,1,1024]{2,1,0:T(1,128)}, u32[]{:S(2)}, u32[]{:S(2)}) collective-permute-start(f32[13,1,1024]{2,1,0:T(1,128)} %get-tuple-element.25), channel_id=1, source_target_pairs={{1,0},{2,1},{3,2},{4,3},{5,4},{6,5},{7,6},{8,7},{9,8},{10,9},{11,1... | collective-permute-start | bytes 159752 | tf_op jit(solution)/shard_map/ppermute | solution.py:22
  348.9 14.1 %collective-permute-start.5 = (f32[13,1,1024]{2,1,0:T(1,128)}, f32[13,1,1024]{2,1,0:T(1,128)}, u32[]{:S(2)}, u32[]{:S(2)}) collective-permute-start(f32[13,1,1024]{2,1,0:T(1,128)} %get-tuple-element.24), channel_id=1, source_target_pairs={{0,1},{1,2},{2,3},{3,4},{4,5},{5,6},{6,7},{7,8},{8,9},{9,10},{10,1... | collective-permute-start | bytes 159752 | tf_op jit(solution)/shard_map/ppermute | solution.py:19
  352.0 27.8 %all-to-all-start.2 = ((f32[16,1,128]{2,1,0:T(1,128)}), f32[16,1,128]{2,1,0:T(1,128)}, u32[]{:S(2)}, u32[]{:S(2)}) async-start(f32[16,1,128]{2,1,0:T(1,128)} %reshape.62), calls=%async_computation.2 | async-start | bytes 16384 | tf_op jit(solution)/shard_map/all_to_all | solution.py:110
  364.3 2.9 copy-start.9
  364.3 2.9 copy-start.11
  367.1 0.8 copy-start.4
  367.1 0.8 copy-start.5
  367.2 0.7 copy-start.15
  367.2 5.0 %copy-start.13 = (s32[64]{0:T(128)S(1)}, s32[64]{0:T(128)}, u32[]{:S(2)}) copy-start(s32[64]{0:T(128)} %get-tuple-element.48) | copy-start | bytes 772
  367.2 10.3 %copy-start.7 = (f32[4]{0:T(128)S(1)}, f32[4]{0:T(128)}, u32[]{:S(2)}) copy-start(f32[4]{0:T(128)} %get-tuple-element.44) | copy-start | bytes 52
  369.1 4.4 %collective-permute-start.6 = (f32[1,1,1024]{2,1,0:T(1,128)S(1)}, f32[1,1,1024]{2,1,0:T(1,128)S(1)}, u32[]{:S(2)}, u32[]{:S(2)}) collective-permute-start(f32[1,1,1024]{2,1,0:T(1,128)S(1)} %get-tuple-element.35), channel_id=1, source_target_pairs={{1,0},{2,1},{3,2},{4,3},{5,4},{6,5},{7,6},{8,7},{9,8},{10,9},{11,1... | collective-permute-start | bytes 12296 | tf_op jit(solution)/shard_map/ppermute | solution.py:22
  372.2 5.2 %collective-permute-start.7 = (f32[1,1,1024]{2,1,0:T(1,128)S(1)}, f32[1,1,1024]{2,1,0:T(1,128)S(1)}, u32[]{:S(2)}, u32[]{:S(2)}) collective-permute-start(f32[1,1,1024]{2,1,0:T(1,128)S(1)} %get-tuple-element.36), channel_id=1, source_target_pairs={{0,1},{1,2},{2,3},{3,4},{4,5},{5,6},{6,7},{7,8},{8,9},{9,10},{10,1... | collective-permute-start | bytes 12296 | tf_op jit(solution)/shard_map/ppermute | solution.py:19
  378.0 1.2 copy-start
  379.3 2.1 collective-permute-start.8
  379.4 5.7 %collective-permute-start.9 = (f32[13,1,1024]{2,1,0:T(1,128)S(1)}, f32[13,1,1024]{2,1,0:T(1,128)S(1)}, u32[]{:S(2)}, u32[]{:S(2)}) collective-permute-start(f32[13,1,1024]{2,1,0:T(1,128)S(1)} %get-tuple-element.20), channel_id=1, source_target_pairs={{0,1},{1,2},{2,3},{3,4},{4,5},{5,6},{6,7},{7,8},{8,9},{9,10},{10,1... | collective-permute-start | bytes 159752 | tf_op jit(solution)/shard_map/ppermute | solution.py:19
  381.3 4.2 %copy-start.1 = (f32[13,32,1024]{2,1,0:T(8,128)S(1)}, f32[13,32,1024]{2,1,0:T(8,128)}, u32[]{:S(2)}) copy-start(f32[13,32,1024]{2,1,0:T(8,128)} %copy-done) | copy-start | bytes 5111812
  389.3 2.0 collective-permute-start.10
  390.0 5.1 %collective-permute-start.11 = (f32[1,1,1024]{2,1,0:T(1,128)S(1)}, f32[1,1,1024]{2,1,0:T(1,128)S(1)}, u32[]{:S(2)}, u32[]{:S(2)}) collective-permute-start(f32[1,1,1024]{2,1,0:T(1,128)S(1)} %get-tuple-element.32), channel_id=1, source_target_pairs={{0,1},{1,2},{2,3},{3,4},{4,5},{5,6},{6,7},{7,8},{8,9},{9,10},{10,1... | collective-permute-start | bytes 12296 | tf_op jit(solution)/shard_map/ppermute | solution.py:19
Sparse Core Ops, SparseCore 0:
  9.8 312.2 all-gather.1
